TPU v7x, 512 devices: a whole 4x4x16 slice. The times are simulated.
512 devices in a mesh: gr: 16 (over z_hi, y, core), gc: 32 (over x, z_lo).
Axes of the slice: x: 4, y: 4, z: 16 (z_hi: 2, z_lo: 8; z = z_hi * 8 + z_lo), core: 2. Of those that a mesh axis runs over, the one named last changes fastest.
Arguments:
- features: bfloat16 [65536, 1024], P(('gr', 'gc')), may hold values from -6 to 6
- weight: bfloat16 [1024, 1024], replicated, may hold values from -0.1875 to 0.1875
- cotangent: bfloat16 [65536, 1024], P(('gr', 'gc')), may hold values from -6 to 6
- block_values: bfloat16 [512, 16, 128, 128], P(('gr', 'gc')), as said below
- block_codes: int32 [512, 16], P(('gr', 'gc')), may hold values from 0 to 511, as said below
- block_count: int32 [512], P(('gr', 'gc')), may hold values from 1 to 16, as said below
Outputs:
- output: float32 [65536, 1024], P(('gr', 'gc'))
- input_grad: float32 [65536, 1024], P(('gr', 'gc'))
- weight_grad: float32 [1024, 1024], P('gc')
Inputs may be any that keep to these rules, and one draw needn't show every extreme that they name: `block_codes`: write code = row * 512 + column. In every slot, row lies in 0 to 0 and column is a block of a slice s + j * 32 with |j| <= 8 (same grid column, at most 8 grid rows away). The codes of the live slots of one slice differ from one another. Every diagonal block (block row equal to block column) is live. The live slots of a slice are its first block_count slots; the entries of later slots are not part of the adjacency. In every draw some slice has all 16 slots live. `block_values`: the adjacency is symmetric: a block is live exactly when its mirror block is, and its entries are the transpose of the mirror's.
All inputs are finite; a program needn't handle non-finite values.
Results may differ from a plain program's by a relative error of at most 0.0045.
Values may be sent and summed in bfloat16 or wider, within the bound.
No kernel may reach another device: no remote copies, remote signals or barrier semaphores. Data moves between devices by JAX's collectives and lax.ppermute only.
A program may use at most 64 MiB of HBM per device.

v0:
```python
import jax
import jax.numpy as jnp
from jax import lax
from jax.sharding import PartitionSpec as P


def dense_tile(row_index, block_index, active, values, piece_blocks, row_blocks):
    block_size = values.shape[-1]
    select_col = (block_index[:, None] == jnp.arange(piece_blocks)[None, :]) & active[:, None]
    select_row = row_index[:, None] == jnp.arange(row_blocks)[None, :]
    tiled = jnp.einsum(
        "ka,km,kij->aimj",
        select_row.astype(jnp.bfloat16),
        select_col.astype(jnp.bfloat16),
        values,
        preferred_element_type=jnp.float32,
    )
    return tiled.astype(jnp.bfloat16).reshape(row_blocks * block_size, piece_blocks * block_size)


def aggregate(source, layout):
    row_index, block_index, active, values = layout
    node_rows = source.shape[0]
    block_size = values.shape[-1]
    row_blocks = node_rows // block_size
    portion = lax.all_gather(source, "gr", axis=0, tiled=True)
    tile = dense_tile(
        row_index, block_index, active, values, portion.shape[0] // block_size, row_blocks
    )
    return jnp.dot(tile, portion, preferred_element_type=jnp.float32)


def local(features, weight, cotangent, block_values, block_codes, block_count):
    node_rows = features.shape[0]
    block_size = block_values.shape[-1]
    row_blocks = node_rows // block_size
    grid_cols = lax.axis_size("gc")
    grid_rows = lax.axis_size("gr")
    all_blocks = row_blocks * grid_rows * grid_cols
    slot_codes = block_codes[0]
    row_index = slot_codes // all_blocks
    column_block = slot_codes % all_blocks
    block_index = column_block // row_blocks // grid_cols * row_blocks + column_block % row_blocks
    active = jnp.arange(slot_codes.shape[0]) < block_count[0]
    layout = (row_index, block_index, active, block_values[0])
    projected = jnp.dot(features, weight, preferred_element_type=jnp.float32).astype(jnp.bfloat16)
    summed = aggregate(projected, layout)
    sigmoid = jax.nn.sigmoid(summed)
    output = summed * sigmoid
    act_slope = (cotangent.astype(jnp.float32) * sigmoid * (1.0 + summed * (1.0 - sigmoid))).astype(
        jnp.bfloat16
    )
    back_grad = aggregate(act_slope, layout).astype(jnp.bfloat16)
    input_grad = lax.dot_general(
        back_grad, weight, (((1,), (1,)), ((), ())), preferred_element_type=jnp.float32
    )
    grad_scale = (node_rows * grid_rows * grid_cols) ** (-0.5)
    partial_grad = (
        lax.dot_general(
            features, back_grad, (((0,), (0,)), ((), ())), preferred_element_type=jnp.float32
        )
        * grad_scale
    )
    row_share = lax.psum_scatter(partial_grad, "gc", scatter_dimension=0, tiled=True)
    weight_grad = lax.psum(row_share, "gr")
    return (output, input_grad, weight_grad)


def solution(mesh):
    in_specs = (
        P(("gr", "gc"), None),
        P(),
        P(("gr", "gc"), None),
        P(("gr", "gc"), None, None, None),
        P(("gr", "gc"), None),
        P(("gr", "gc")),
    )
    out_specs = (P(("gr", "gc"), None), P(("gr", "gc"), None), P("gc", None))
    return jax.shard_map(local, mesh=mesh, in_specs=in_specs, out_specs=out_specs, check_vma=False)
```

profile of v0, /device:TPU:1, one launch (start us, length us, event | category | flops | bytes accessed | tf_op | source)
XLA Modules:
  0.0 770.5 jit_solution(15007061973408233624)
XLA Ops:
  7.2 0.0 all-gather.3.cloned.1.call-start
  7.2 1.5 copy-done
  8.8 2.1 convolution_convert_fusion.1
  10.9 0.0 all-gather.3.cloned.1.call-update
  10.9 0.0 all-gather.5.cloned.1.call-start
  11.6 0.7 and_select_fusion.1
  12.3 0.7 compare_convert_fusion
  12.9 1.5 convolution_convert_fusion
  14.4 122.6 %all-gather.3.cloned.1.call-done = bf16[2048,1024]{1,0:T(8,128)(2,1)} async-done(((bf16[128,1024]{1,0:T(8,128)(2,1)}), bf16[2048,1024]{1,0:T(8,128)(2,1)}) %all-gather.3.cloned.1.call-update) | async-done | bytes 4194320 | tf_op jit(solution)/shard_map/all_gather | solution.py:26
  137.0 4.0 multiply_convert_fusion
  141.0 0.0 all-gather.5.cloned.1.call-update
  141.0 0.0 reduce-scatter.4.cloned.1.call-start
  141.1 112.4 %all-gather.5.cloned.1.call-done = bf16[2048,1024]{1,0:T(8,128)(2,1)} async-done(((bf16[128,1024]{1,0:T(8,128)(2,1)}), bf16[2048,1024]{1,0:T(8,128)(2,1)}) %all-gather.5.cloned.1.call-update) | async-done | bytes 4194320 | tf_op jit(solution)/shard_map/all_gather | solution.py:26
  253.5 2.9 convolution_convert_fusion.2
  256.4 2.7 multiply_bitcast_fusion
  259.1 5.4 copy.13
  264.5 0.0 reduce-scatter.4.cloned.1.call-update
  264.5 0.0 all-reduce.2.cloned.1.call-start
  264.6 222.1 %reduce-scatter.4.cloned.1.call-done = f32[32,1024]{1,0:T(8,128)} async-done(((f32[1024,1024]{1,0:T(8,128)}), f32[32,1024]{1,0:T(8,128)}) %reduce-scatter.4.cloned.1.call-update) | async-done | bytes 131088
  486.6 1.9 copy.14
  488.5 0.0 all-reduce.2.cloned.1.call-update
  488.6 1.6 fusion.16
  490.2 271.9 %all-reduce.2.cloned.1.call-done = f32[32,1024]{0,1:T(8,128)} async-done(((f32[32,1024]{0,1:T(8,128)}), f32[32,1024]{0,1:T(8,128)}) %all-reduce.2.cloned.1.call-update) | async-done | bytes 131088 | tf_op jit(solution)/shard_map/psum | solution.py:65
  762.1 1.9 copy.12
  (3 shorter events, 0.0 us)
Async XLA Ops:
  7.2 1.6 copy-start
  7.2 129.8 %all-gather.3.cloned.1.call-start = ((), (), s32[]{:S(2)}) async-start(), calls=%async_computation.1 | async-start | bytes 4456448 | tf_op jit(solution)/shard_map/all_gather | solution.py:26
  10.9 242.6 %all-gather.5.cloned.1.call-start = ((), (), s32[]{:S(2)}) async-start(), calls=%async_computation.2 | async-start | bytes 4456448 | tf_op jit(solution)/shard_map/all_gather | solution.py:26
  141.0 115.4 %copy-start.1 = (bf16[128,1024]{1,0:T(8,128)(2,1)S(1)}, bf16[128,1024]{1,0:T(8,128)(2,1)}, u32[]{:S(2)}) copy-start(bf16[128,1024]{1,0:T(8,128)(2,1)} %param.6) | copy-start | bytes 786436
  141.0 345.6 %reduce-scatter.4.cloned.1.call-start = ((), (), s32[]{:S(2)}) async-start(), calls=%async_computation.4 | async-start | bytes 4325376
  264.5 497.6 %all-reduce.2.cloned.1.call-start = ((), (), s32[]{:S(2)}) async-start(), calls=%async_computation.3 | async-start | bytes 1048576 | tf_op jit(solution)/shard_map/psum | solution.py:65
Sparse Core Ops, SparseCore 0:
  11.9 125.0 all-gather.2
  141.1 112.3 all-gather.4
  264.6 221.9 reduce-scatter.3
  489.4 272.6 all-reduce.1
where the time goes:
time: 771 us; the launch traced here: 770 us
  waiting for transfers between devices  729 us (95%)
  matrix products  14.8 us (2%)
  between operations  14.4 us (2%)
  local copies, waits for them, and re-layouts  10.7 us (1%)
    psum x1, waiting for transfers between devices, local(): weight_grad = lax.psum(row_share, 'gr')  272 us
    all_gather x2, waiting for transfers between devices, aggregate(): portion = lax.all_gather(source, 'gr', axis=0, tiled=True)  235 us
    unnamed x5, waiting for transfers between devices  222 us
  transfers between devices with their start and end apart: 4, of which 4 were waited for; matrix products, arithmetic and copies ran while one was open for 1% of the time, Pallas kernels for 0%

commit v1 on v0

--- a/solution.py
+++ b/solution.py
@@ -62,7 +62,8 @@
         * grad_scale
     )
     row_share = lax.psum_scatter(partial_grad, "gc", scatter_dimension=0, tiled=True)
-    weight_grad = lax.psum(row_share, "gr")
+    pieces = lax.all_gather(row_share, "gr")
+    weight_grad = jnp.sum(pieces, axis=0)
     return (output, input_grad, weight_grad)
 
 

time: 771 us -> 608 us (0.79)
  waiting for transfers between devices: 729 us -> 568 us
    psum x1 -> x0, waiting for transfers between devices: 272 us -> none  [local(): weight_grad = lax.psum(row_share, 'gr')]
    reduce_scatter x0 -> x1, waiting for transfers between devices: none -> 222 us  [local(): lax.psum_scatter(partial_grad, 'gc', scatter_dimension=0, tiled=True)]
    unnamed x5 -> x4, waiting for transfers between devices: 222 us -> 0.07 us
    all_gather x0 -> x1, waiting for transfers between devices: none -> 111 us  [local(): pieces = lax.all_gather(row_share, 'gr')]
where the time goes in v1:
time: 608 us
  waiting for transfers between devices  568 us (93%)
  matrix products  14.8 us (2%)
  between operations  14.4 us (2%)
  local copies, waits for them, and re-layouts  6.9 us (1%)
    all_gather x2, waiting for transfers between devices, aggregate(): portion = lax.all_gather(source, 'gr', axis=0, tiled=True)  235 us
    reduce_scatter x1, waiting for transfers between devices, local(): lax.psum_scatter(partial_grad, 'gc', scatter_dimension=0, tiled=True)  222 us
    all_gather x1, waiting for transfers between devices, local(): pieces = lax.all_gather(row_share, 'gr')  111 us
  transfers between devices with their start and end apart: 4, of which 4 were waited for; matrix products, arithmetic and copies ran while one was open for 1% of the time, Pallas kernels for 0%

profile of v1, /device:TPU:1, one launch (start us, length us, event | category | flops | bytes accessed | tf_op | source)
XLA Modules:
  0.0 608.0 jit_solution(6698389082501045366)
XLA Ops:
  7.2 0.0 copy-start
  7.2 0.0 all-gather.5.cloned.1.call-start
  7.2 1.5 copy-done
  8.8 2.1 convolution_convert_fusion.1
  10.9 0.0 all-gather.5.cloned.1.call-update
  10.9 0.0 all-gather.7.cloned.1.call-start
  11.6 0.7 and_select_fusion.1
  12.3 0.7 compare_convert_fusion
  12.9 1.5 convolution_convert_fusion
  14.4 122.6 %all-gather.5.cloned.1.call-done = bf16[2048,1024]{1,0:T(8,128)(2,1)} async-done(((bf16[128,1024]{1,0:T(8,128)(2,1)}), bf16[2048,1024]{1,0:T(8,128)(2,1)}) %all-gather.5.cloned.1.call-update) | async-done | bytes 4194320 | tf_op jit(solution)/shard_map/all_gather | solution.py:26
  137.0 4.0 multiply_convert_fusion
  141.0 0.0 all-gather.7.cloned.1.call-update
  141.0 0.0 reduce-scatter.4.cloned.1.call-start
  141.1 112.4 %all-gather.7.cloned.1.call-done = bf16[2048,1024]{1,0:T(8,128)(2,1)} async-done(((bf16[128,1024]{1,0:T(8,128)(2,1)}), bf16[2048,1024]{1,0:T(8,128)(2,1)}) %all-gather.7.cloned.1.call-update) | async-done | bytes 4194320 | tf_op jit(solution)/shard_map/all_gather | solution.py:26
  253.5 2.9 convolution_convert_fusion.2
  256.4 2.7 multiply_bitcast_fusion
  259.1 5.4 copy.14
  264.5 0.0 reduce-scatter.4.cloned.1.call-update
  264.5 0.0 all-gather.9.cloned.1.call-start
  264.6 222.1 %reduce-scatter.4.cloned.1.call-done = f32[32,1024]{1,0:T(8,128)} async-done(((f32[1024,1024]{1,0:T(8,128)}), f32[32,1024]{1,0:T(8,128)}) %reduce-scatter.4.cloned.1.call-update) | async-done | bytes 131088 | tf_op jit(solution)/shard_map/reduce_scatter | solution.py:64
  486.6 0.0 all-gather.9.cloned.1.call-update
  486.7 1.6 fusion.16
  488.3 110.8 %all-gather.9.cloned.1.call-done = f32[512,1024]{1,0:T(8,128)} async-done(((f32[32,1024]{1,0:T(8,128)}), f32[512,1024]{1,0:T(8,128)}) %all-gather.9.cloned.1.call-update) | async-done | bytes 2097168 | tf_op jit(solution)/shard_map/all_gather | solution.py:65
  599.1 2.4 reduce_sum.9
  (2 shorter events, 0.0 us)
Async XLA Ops:
  7.2 1.6 copy-start
  7.2 129.8 %all-gather.5.cloned.1.call-start = ((), (), s32[]{:S(2)}) async-start(), calls=%async_computation.1 | async-start | bytes 4456448 | tf_op jit(solution)/shard_map/all_gather | solution.py:26
  10.9 242.6 %all-gather.7.cloned.1.call-start = ((), (), s32[]{:S(2)}) async-start(), calls=%async_computation.2 | async-start | bytes 4456448 | tf_op jit(solution)/shard_map/all_gather | solution.py:26
  141.0 115.4 %copy-start.1 = (bf16[128,1024]{1,0:T(8,128)(2,1)S(1)}, bf16[128,1024]{1,0:T(8,128)(2,1)}, u32[]{:S(2)}) copy-start(bf16[128,1024]{1,0:T(8,128)(2,1)} %param.6) | copy-start | bytes 786436
  141.0 345.6 %reduce-scatter.4.cloned.1.call-start = ((), (), s32[]{:S(2)}) async-start(), calls=%async_computation.4 | async-start | bytes 4325376 | tf_op jit(solution)/shard_map/reduce_scatter | solution.py:64
  264.5 334.6 %all-gather.9.cloned.1.call-start = ((), (), s32[]{:S(2)}) async-start(), calls=%async_computation.3 | async-start | bytes 2228224 | tf_op jit(solution)/shard_map/all_gather | solution.py:65
Sparse Core Ops, SparseCore 0:
  11.9 125.0 all-gather.4
  141.1 112.3 all-gather.6
  264.6 221.9 reduce-scatter.3
  489.8 109.2 all-gather.8

commit v2 on v0

--- a/solution.py
+++ b/solution.py
@@ -23,7 +23,16 @@
     node_rows = source.shape[0]
     block_size = values.shape[-1]
     row_blocks = node_rows // block_size
-    portion = lax.all_gather(source, "gr", axis=0, tiled=True)
+    trace_shifts_all = lambda slab_in, axis_id, along_dim: jnp.concatenate(
+        lax.all_to_all(
+            jnp.stack([slab_in for _ in range(lax.axis_size(axis_id))], axis=0),
+            axis_id,
+            split_axis=0,
+            concat_axis=0,
+        ),
+        along_dim,
+    )
+    portion = trace_shifts_all(source, "gr", 0)
     tile = dense_tile(
         row_index, block_index, active, values, portion.shape[0] // block_size, row_blocks
     )

time: 771 us -> 952 us (1.23)
  blocking collectives: 0 us -> 140 us
  waiting for transfers between devices: 729 us -> 753 us
  starting transfers between devices: 0.16 us -> 19.4 us
    all_gather x2 -> x0, waiting for transfers between devices: 235 us -> none  [aggregate(): portion = lax.all_gather(source, 'gr', axis=0, tiled=True)]
    unnamed x5 -> x3, waiting for transfers between devices: 222 us -> 387 us
    all_to_all x0 -> x1, blocking collectives: none -> 140 us  [aggregate(): lax.all_to_all(jnp.stack([slab_in for _ in range(lax.axis_size(axis_id))]...]
    all_to_all x0 -> x1, waiting for transfers between devices: none -> 95.1 us  [aggregate(): lax.all_to_all(jnp.stack([slab_in for _ in range(lax.axis_size(axis_id))]...]
    all_to_all x0 -> x1, starting transfers between devices: none -> 19.4 us  [aggregate(): lax.all_to_all(jnp.stack([slab_in for _ in range(lax.axis_size(axis_id))]...]
  transfers between devices with their start and end apart: 4 -> 3, of which waited for: 4 -> 3; matrix products, arithmetic and copies ran while one was open for 1% -> 0% of each run, Pallas kernels for 0% -> 0%
where the time goes in v2:
time: 952 us
  waiting for transfers between devices  753 us (79%)
  blocking collectives  140 us (15%)
  starting transfers between devices  19.4 us (2%)
  between operations  14.8 us (2%)
  local copies, waits for them, and re-layouts  14 us (1%)
  matrix products  10.8 us (1%)
    unnamed x3, waiting for transfers between devices  387 us
    psum x1, waiting for transfers between devices, local(): weight_grad = lax.psum(row_share, 'gr')  271 us
    all_to_all x1, blocking collectives, aggregate(): lax.all_to_all(jnp.stack([slab_in for _ in range(lax.axis_size(axis_id))]...  140 us
    all_to_all x1, waiting for transfers between devices, aggregate(): lax.all_to_all(jnp.stack([slab_in for _ in range(lax.axis_size(axis_id))]...  95.1 us
    all_to_all x1, starting transfers between devices, aggregate(): lax.all_to_all(jnp.stack([slab_in for _ in range(lax.axis_size(axis_id))]...  19.4 us
  transfers between devices with their start and end apart: 3, of which 3 were waited for; matrix products, arithmetic and copies ran while one was open for 0% of the time, Pallas kernels for 0%

profile of v2, /device:TPU:1, one launch (start us, length us, event | category | flops | bytes accessed | tf_op | source)
XLA Modules:
  0.0 951.7 jit_solution(14132679531708192601)
XLA Ops:
  7.2 0.0 copy-start
  7.2 1.6 copy-done
  8.8 1.4 convolution_convert_fusion.1
  10.2 2.5 stack.4
  12.7 19.4 %all-to-all-start = ((bf16[16,128,1024]{2,1,0:T(8,128)(2,1)}), bf16[16,128,1024]{2,1,0:T(8,128)(2,1)}, u32[]{:S(2)}, u32[]{:S(2)}) async-start(bf16[16,128,1024]{2,1,0:T(8,128)(2,1)} %stack.4), calls=%async_computation | async-start | bytes 8388608 | tf_op jit(solution)/shard_map/all_to_all | solution.py:27
  32.0 0.0 reduce-scatter.4.cloned.1.call-start
  32.7 0.0 copy-done.3
  32.8 0.4 convolution_convert_fusion
  33.2 95.1 %all-to-all-done = bf16[16,128,1024]{2,1,0:T(8,128)(2,1)} async-done(((bf16[16,128,1024]{2,1,0:T(8,128)(2,1)}), bf16[16,128,1024]{2,1,0:T(8,128)(2,1)}, u32[]{:S(2)}, u32[]{:S(2)}) %all-to-all-start) | async-done | bytes 4194336 | tf_op jit(solution)/shard_map/all_to_all | solution.py:27
  128.3 3.9 multiply_convert_fusion
  132.2 0.5 stack.5
  132.7 139.6 %all_to_all.10 = bf16[16,128,1024]{2,1,0:T(8,128)(2,1)S(1)} all-to-all(bf16[16,128,1024]{2,1,0:T(8,128)(2,1)S(1)} %stack.5), channel_id=1, replica_groups=mesh['gr'=16,'gc'=32] {'gr'}, dimensions={0} | all-to-all | bytes 8388608 | tf_op jit(solution)/shard_map/all_to_all | solution.py:27
  272.3 0.7 convolution_convert_fusion.2
  273.1 0.2 copy-done.1
  273.3 2.7 multiply_bitcast_fusion
  276.0 5.4 copy.13
  281.3 0.0 reduce-scatter.4.cloned.1.call-update
  281.4 0.0 all-reduce.2.cloned.1.call-start
  281.4 386.5 %reduce-scatter.4.cloned.1.call-done = f32[32,1024]{1,0:T(8,128)} async-done(((f32[1024,1024]{1,0:T(8,128)}), f32[32,1024]{1,0:T(8,128)}) %reduce-scatter.4.cloned.1.call-update) | async-done | bytes 131088
  667.9 1.9 copy.14
  669.9 0.0 all-reduce.2.cloned.1.call-update
  669.9 1.6 fusion.16
  671.5 271.5 %all-reduce.2.cloned.1.call-done = f32[32,1024]{0,1:T(8,128)} async-done(((f32[32,1024]{0,1:T(8,128)}), f32[32,1024]{0,1:T(8,128)}) %all-reduce.2.cloned.1.call-update) | async-done | bytes 131088 | tf_op jit(solution)/shard_map/psum | solution.py:74
  943.0 1.9 copy.12
  (8 shorter events, 0.0 us)
Async XLA Ops:
  7.2 1.6 copy-start
  12.7 20.1 %copy-start.3 = (s32[1,16]{1,0:T(1,128)S(1)}, s32[1,16]{1,0:T(1,128)}, u32[]{:S(2)}) copy-start(s32[1,16]{1,0:T(1,128)} %param.10) | copy-start | bytes 196
  12.7 20.1 %copy-start.2 = (bf16[1,16,128,128]{3,2,1,0:T(8,128)(2,1)S(1)}, bf16[1,16,128,128]{3,2,1,0:T(8,128)(2,1)}, u32[]{:S(2)}) copy-start(bf16[1,16,128,128]{3,2,1,0:T(8,128)(2,1)} %param.9) | copy-start | bytes 1572868
  12.7 115.6 %copy-start.4 = (bf16[128,1024]{1,0:T(8,128)(2,1)S(1)}, bf16[128,1024]{1,0:T(8,128)(2,1)}, u32[]{:S(2)}) copy-start(bf16[128,1024]{1,0:T(8,128)(2,1)} %param.8) | copy-start | bytes 786436
  12.7 115.6 %all-to-all-start = ((bf16[16,128,1024]{2,1,0:T(8,128)(2,1)}), bf16[16,128,1024]{2,1,0:T(8,128)(2,1)}, u32[]{:S(2)}, u32[]{:S(2)}) async-start(bf16[16,128,1024]{2,1,0:T(8,128)(2,1)} %stack.4), calls=%async_computation | async-start | bytes 8388608 | tf_op jit(solution)/shard_map/all_to_all | solution.py:27
  32.0 635.9 %reduce-scatter.4.cloned.1.call-start = ((), (), s32[]{:S(2)}) async-start(), calls=%async_computation.4 | async-start | bytes 4325376
  272.3 1.0 copy-start.1
  281.4 661.6 %all-reduce.2.cloned.1.call-start = ((), (), s32[]{:S(2)}) async-start(), calls=%async_computation.3 | async-start | bytes 1048576 | tf_op jit(solution)/shard_map/psum | solution.py:74
Sparse Core Ops, SparseCore 0:
  281.5 386.4 reduce-scatter.3
  670.8 272.0 all-reduce.1
